TPU v7x, 32 devices: a whole 2x2x4 slice. The times are simulated.
32 devices in a mesh: dom: 8 (over z, x), slab: 4 (over y, core).
Axes of the slice: x: 2, y: 2, z: 4, core: 2. Of those that a mesh axis runs over, the one named last changes fastest.
Arguments:
- basis_weights: float32 [4, 4, 12288], P(None, 'slab', 'dom'), may hold values from 0 to 1, as said below
- velocity: float32 [3, 4, 12288], P(None, 'slab', 'dom'), may hold values from -6 to 6
- owner_dom: int32 [4, 12288, 1], P('slab', 'dom'), may hold values from 0 to 7; in each aligned block of 1536 rows (0 to 1535, 1536 to 3071, ..., all dimensions but the last counted through in order) at most 384 rows name the same one
- cell_local: int32 [4, 12288], P('slab', 'dom'), may hold values from 0 to 255
- inverse: float32 [16, 4, 2048], P(None, 'slab', 'dom'), may hold values from -0.2 to 1.5
- connectivity: int32 [4, 4, 2048], P(None, 'slab', 'dom'), may hold values from 0 to 2303, as said below
Outputs:
- coefficients: float32 [12, 4, 2048], P(None, 'slab', 'dom')
- node_values: float32 [3, 4, 2048], P(None, 'slab', 'dom')
Inputs may be any that keep to these rules, and one draw needn't show every extreme that they name: `basis_weights`: the four entries of each particle are positive and sum to one. `owner_dom`: among the rows of one device, no owner is named more than 384 times. `connectivity`: the slab move and dom move are each -1, 0 or 1, and the node they name lies inside the domain.
All inputs are finite; a program needn't handle non-finite values.
Results may differ from a plain program's by a relative error of at most 0.00011.
Values sent between devices are 32-bit elements; how exact they have to be, the bound alone decides.
No kernel may reach another device: no remote copies, remote signals or barrier semaphores. Data moves between devices by JAX's collectives and lax.ppermute only.
A program may use at most 64 MiB of HBM per device.

v0:
```python
import math
import jax
import jax.numpy as jnp
import numpy as np
from jax import lax
from jax.sharding import PartitionSpec as P

NODES_DEV = 256
PAIR_FIRST = np.array([0, 0, 0, 0, 1, 1, 1, 2, 2, 3], dtype=np.int32)
PAIR_SECOND = np.array([0, 1, 2, 3, 1, 2, 3, 2, 3, 3], dtype=np.int32)
GRAM_FROM_PAIR = np.array([0, 1, 2, 3, 1, 4, 5, 6, 2, 5, 7, 8, 3, 6, 8, 9], dtype=np.int32)


def from_behind(array, axis, by):
    devices = lax.axis_size(axis)
    pairs = [(i, i + by) for i in range(devices) if 0 <= i + by < devices]
    return lax.ppermute(array, axis, pairs)


def expand_terms(weights, velocities):
    upper_terms = weights[PAIR_FIRST] * weights[PAIR_SECOND]
    moment_terms = (weights[:, None, :] * velocities[None, :, :]).reshape(12, -1)
    return jnp.concatenate([upper_terms, moment_terms], axis=0)


def onehot_sum(values, segment_ids, segment_count):
    total = segment_ids.shape[0]
    row_count = values.shape[0]
    limit = max(128, 2097152 // segment_count)
    block = math.gcd(total, limit)
    rounds = total // block
    value_blocks = jnp.transpose(values.reshape(row_count, rounds, block), (1, 0, 2))
    id_blocks = segment_ids.reshape(rounds, block)
    columns = jnp.arange(segment_count, dtype=jnp.int32)

    def accumulate(carry, items):
        value_block, id_block = items
        table = (id_block[:, None] == columns[None, :]).astype(jnp.float32)
        return (
            carry
            + jnp.dot(
                value_block,
                table,
                precision=lax.Precision.HIGHEST,
                preferred_element_type=jnp.float32,
            ),
            None,
        )

    start = jnp.zeros((row_count, segment_count), jnp.float32)
    result, unused = lax.scan(accumulate, start, (value_blocks, id_blocks))
    return result


def per_device(basis_weights, velocity, owner_dom, cell_local, inverse, connectivity):
    particles = basis_weights.shape[2]
    cell_count = inverse.shape[2]
    dom_count = lax.axis_size("dom")
    capacity = 2 * particles // dom_count
    slot_count = dom_count * capacity
    destination = owner_dom.reshape(particles)
    sort_order = jnp.argsort(destination, stable=True)
    ranked = destination[sort_order]
    starts = jnp.searchsorted(ranked, jnp.arange(dom_count, dtype=jnp.int32))
    slot_index = ranked * capacity + jnp.arange(particles, dtype=jnp.int32) - starts[ranked]
    weights = basis_weights[:, 0]
    velocities = velocity[:, 0]
    cell_float = cell_local.astype(jnp.float32)
    payload = jnp.concatenate([weights, velocities, cell_float], axis=0)
    empty = jnp.zeros((payload.shape[0], slot_count), jnp.float32)
    outgoing = empty.at[:, slot_index].set(payload[:, sort_order])
    arrived = lax.all_to_all(outgoing, "dom", split_axis=1, concat_axis=1, tiled=True)
    products = expand_terms(arrived[:4], arrived[4:7])
    cell_index = arrived[7].astype(jnp.int32)
    totals = onehot_sum(products, cell_index, cell_count)
    gram_full = totals[:10][GRAM_FROM_PAIR].reshape(4, 4, cell_count)
    moment = totals[10:].reshape(4, 3, cell_count)
    matrix = inverse[:, 0].reshape(4, 4, cell_count)
    first_pass = jnp.sum(matrix[:, :, None, :] * moment[None], axis=1)
    residual_part = moment - jnp.sum(gram_full[:, :, None, :] * first_pass[None], axis=1)
    solved = first_pass + jnp.sum(matrix[:, :, None, :] * residual_part[None], axis=1)
    coefficients = solved.reshape(12, 1, cell_count)
    node_count = NODES_DEV
    bucket = connectivity[:, 0]
    corner_values = jnp.transpose(solved, (1, 0, 2)).reshape(3, 4 * cell_count)
    local_sums = onehot_sum(corner_values, bucket.reshape(-1), 9 * node_count).reshape(
        3, 3, 3, node_count
    )
    from_below = from_behind(local_sums[:, :, 2], "dom", 1)
    from_above = from_behind(local_sums[:, :, 0], "dom", -1)
    merged = local_sums[:, :, 1] + from_below + from_above
    slab_below = from_behind(merged[:, 2], "slab", 1)
    slab_above = from_behind(merged[:, 0], "slab", -1)
    node_values = (merged[:, 1] + slab_below + slab_above).reshape(3, 1, node_count)
    return (coefficients, node_values)


def solution(mesh):
    in_specs = (
        P(None, "slab", "dom"),
        P(None, "slab", "dom"),
        P("slab", "dom", None),
        P("slab", "dom"),
        P(None, "slab", "dom"),
        P(None, "slab", "dom"),
    )
    out_specs = (P(None, "slab", "dom"), P(None, "slab", "dom"))
    return jax.shard_map(
        per_device, mesh=mesh, in_specs=in_specs, out_specs=out_specs, check_vma=False
    )
```

profile of v0, /device:TPU:1, one launch (start us, length us, event | category | flops | bytes accessed | tf_op | source)
XLA Modules:
  0.0 230.3 jit_solution(17716945003019900651)
XLA Ops:
  0.6 0.7 reduce
  1.4 5.0 %sort.17 = (s32[1536]{0:T(1024)}, s32[1536]{0:T(1024)S(1)}) sort(s32[1536]{0:T(1024)S(1)} %reduce, s32[1536]{0:T(1024)S(1)} %iota.17), dimensions={0}, to_apply=%region_0.0 | sort | flops 16896 | bytes 24576 | tf_op jit(solution)/shard_map/jit(argsort)/sort | solution.py:62
  6.4 8.4 %gather_fusion.1 = s32[1536]{0:T(1024)S(1)} fusion(s32[1536]{0:T(1024)S(1)} %reduce, s32[2048]{0:T(1024)S(1)} %pad_clamp_fusion.1), kind=kCustom, calls=%fused_computation.1 | custom fusion | bytes 18432 | tf_op jit(solution)/shard_map/gather | solution.py:63
  14.9 7.6 %while.46 = (s32[]{:T(128)}, u32[8]{0:T(128)S(1)}, u32[8]{0:T(128)S(1)}, s32[1536]{0:T(1024)S(1)}, s32[]{:T(128)}, /*index=5*/s32[]{:T(128)}, s32[]{}) while((s32[]{:T(128)}, u32[8]{0:T(128)S(1)}, u32[8]{0:T(128)S(1)}, s32[1536]{0:T(1024)S(1)}, s32[]{:T(128)}, /*index=5*/s32[]{:T(128)}, s32[]{}) %tuple.91), condition=%wide.region_2.3_spmd.clone, body=%wide.region_1.2_spmd.clone.sunk | while | flops 1132 | bytes 4580 | solution.py:64
  14.9 0.6 gather_fusion
  16.3 0.6 gather_fusion
  17.7 0.6 gather_fusion
  22.5 0.7 fusion.28
  23.2 4.4 %fusion.21 = s32[1536]{0:T(1024)S(1)} fusion(s32[]{:T(128)} %bitcast.1, s32[]{:T(128)} %bitcast.2, s32[]{:T(128)} %bitcast.3, s32[]{:T(128)} %bitcast.4, s32[]{:T(128)} %bitcast.5, s32[]{:T(128)} %bitcast.7, s32[]{:T(128)} %bitcast.6, s32[1536]{0:T(1024)S(1)} %get-tuple-element.381), kind=kLoop, calls=%fused_computation.60 | loop fusion | flops 23040 | bytes 12316 | tf_op jit(solution)/shard_map/gather | solution.py:65
  27.7 0.7 broadcast_select_fusion.2
  28.8 10.0 %scatter_custom_fusion = f32[8,3072]{0,1:T(8,128)S(1)} fusion(s32[1536]{0:T(1024)S(1)} %fusion.22, f32[8,1536]{0,1:T(8,128)S(1)} %copy.55, s32[2048]{0:T(1024)S(1)} %pad_clamp_fusion.1, f32[]{:T(128)} %constant.69.clone.1), kind=kCustom, calls=%fused_computation.31 | custom fusion | bytes 98308 | tf_op jit(solution)/shard_map/scatter | solution.py:71
  38.8 1.1 copy.56
  39.9 6.4 %all-to-all-start = ((f32[8,8,384]{2,0,1:T(8,128)}), f32[8,8,384]{2,0,1:T(8,128)S(1)}, u32[]{:S(2)}, u32[]{:S(2)}) async-start(f32[8,8,384]{2,0,1:T(8,128)} %copy.56), calls=%async_computation | async-start | bytes 196608 | tf_op jit(solution)/shard_map/all_to_all | solution.py:72
  46.6 5.7 %all-to-all-done = f32[8,8,384]{2,0,1:T(8,128)S(1)} async-done(((f32[8,8,384]{2,0,1:T(8,128)}), f32[8,8,384]{2,0,1:T(8,128)S(1)}, u32[]{:S(2)}, u32[]{:S(2)}) %all-to-all-start) | async-done | bytes 98336 | tf_op jit(solution)/shard_map/all_to_all | solution.py:72
  54.0 2.0 while.47
  56.9 0.8 reshape_reshape.3
  57.6 3.2 %copy.62 = f32[512,3,2]{1,2,0:T(2,128)S(1)} copy(f32[512,3,2]{2,0,1:T(8,128)S(1)} %bitcast.70) | data formatting | bytes 24576
  60.9 150.9 %while.48 = (s32[]{:T(128)}, f32[3,2304]{1,0:T(4,128)S(1)}, f32[512,3,2]{1,2,0:T(2,128)S(1)}, s32[512,2]{1,0:T(8,128)S(1)}, s32[]{:T(128)}, /*index=5*/s32[]{:T(128)}) while((s32[]{:T(128)}, f32[3,2304]{1,0:T(4,128)S(1)}, f32[512,3,2]{1,2,0:T(2,128)S(1)}, s32[512,2]{1,0:T(8,128)S(1)}, s32[]{:T(128)}, /*index=5*/s32[]{:T(128)}) %tuple.97), condition=%wide.region_10.11_spmd.clone, body=%wide.region_9.10_spmd.clone.sunk | while | flops 184323 | bytes 66151 | solution.py:51
  211.8 1.8 collective-permute-start
  213.7 1.3 collective-permute-start.1
  215.0 3.1 %collective-permute-done.1 = f32[3,3,256]{2,1,0:T(4,128)S(1)} collective-permute-done((f32[3,3,256]{2,1,0:T(4,128)S(1)}, f32[3,3,256]{2,1,0:T(4,128)S(1)}, u32[]{:S(2)}, u32[]{:S(2)}) %collective-permute-start.1) | collective-permute-done | bytes 9248 | tf_op jit(solution)/shard_map/ppermute | solution.py:17
  218.2 6.6 %collective-permute-start.2 = (f32[3,256]{1,0:T(4,128)S(1)}, f32[3,256]{1,0:T(4,128)S(1)}, u32[]{:S(2)}, u32[]{:S(2)}) collective-permute-start(f32[3,256]{1,0:T(4,128)S(1)} %bitcast.78), channel_id=1, source_target_pairs={{0,1},{1,2},{2,3},{4,5},{5,6},{6,7},{8,9},{9,10},{10,11},{12,13},{... | collective-permute-start | bytes 9224 | tf_op jit(solution)/shard_map/ppermute | solution.py:17
  224.8 1.9 collective-permute-start.3
  227.3 2.4 %collective-permute-done.3 = f32[3,256]{1,0:T(4,128)S(1)} collective-permute-done((f32[3,256]{1,0:T(4,128)S(1)}, f32[3,256]{1,0:T(4,128)S(1)}, u32[]{:S(2)}, u32[]{:S(2)}) %collective-permute-start.3) | collective-permute-done | bytes 3104 | tf_op jit(solution)/shard_map/ppermute | solution.py:17
  (1150 shorter events, 151.0 us)
Async XLA Ops:
  14.8 13.5 %copy-start.1 = (f32[3,1,1536]{2,1,0:T(1,128)S(1)}, f32[3,1,1536]{2,1,0:T(1,128)}, u32[]{:S(2)}) copy-start(f32[3,1,1536]{2,1,0:T(1,128)} %param.19) | copy-start | bytes 55300
  14.8 13.6 %copy-start = (f32[4,1,1536]{2,1,0:T(1,128)S(1)}, f32[4,1,1536]{2,1,0:T(1,128)}, u32[]{:S(2)}) copy-start(f32[4,1,1536]{2,1,0:T(1,128)} %param.18) | copy-start | bytes 73732
  14.8 13.6 %copy-start.3 = (s32[1,1536]{1,0:T(1,128)S(1)}, s32[1,1536]{1,0:T(1,128)}, u32[]{:S(2)}) copy-start(s32[1,1536]{1,0:T(1,128)} %param.21) | copy-start | bytes 18436
  28.7 17.5 %copy-start.7 = (s32[10]{0:T(128)S(1)}, s32[10]{0:T(128)}, u32[]{:S(2)}) copy-start(s32[10]{0:T(128)} %constant.99) | copy-start | bytes 124
  28.8 17.5 %copy-start.2 = (f32[16,1,256]{2,1,0:T(1,128)S(1)}, f32[16,1,256]{2,1,0:T(1,128)}, u32[]{:S(2)}) copy-start(f32[16,1,256]{2,1,0:T(1,128)} %param.22) | copy-start | bytes 49156
  28.8 17.6 %copy-start.4 = (s32[4,1,256]{2,1,0:T(1,128)S(1)}, s32[4,1,256]{2,1,0:T(1,128)}, u32[]{:S(2)}) copy-start(s32[4,1,256]{2,1,0:T(1,128)} %param.23) | copy-start | bytes 12292
  28.8 17.8 %copy-start.6 = (s32[10]{0:T(128)S(1)}, s32[10]{0:T(128)}, u32[]{:S(2)}) copy-start(s32[10]{0:T(128)} %constant.100) | copy-start | bytes 124
  28.8 17.8 %copy-start.5 = (s32[16]{0:T(128)S(1)}, s32[16]{0:T(128)}, u32[]{:S(2)}) copy-start(s32[16]{0:T(128)} %constant.101) | copy-start | bytes 196
  39.9 12.4 %all-to-all-start = ((f32[8,8,384]{2,0,1:T(8,128)}), f32[8,8,384]{2,0,1:T(8,128)S(1)}, u32[]{:S(2)}, u32[]{:S(2)}) async-start(f32[8,8,384]{2,0,1:T(8,128)} %copy.56), calls=%async_computation | async-start | bytes 196608 | tf_op jit(solution)/shard_map/all_to_all | solution.py:72
  211.8 3.1 %collective-permute-start = (f32[3,3,256]{2,1,0:T(4,128)S(1)}, f32[3,3,256]{2,1,0:T(4,128)S(1)}, u32[]{:S(2)}, u32[]{:S(2)}) collective-permute-start(f32[3,3,256]{2,1,0:T(4,128)S(1)} %bitcast.76), channel_id=1, source_target_pairs={{0,4},{4,8},{8,12},{12,16},{16,20},{20,24},{24,28},{1,5},{5,9},{9,... | collective-permute-start | bytes 27656 | tf_op jit(solution)/shard_map/ppermute | solution.py:17
  213.7 4.4 %collective-permute-start.1 = (f32[3,3,256]{2,1,0:T(4,128)S(1)}, f32[3,3,256]{2,1,0:T(4,128)S(1)}, u32[]{:S(2)}, u32[]{:S(2)}) collective-permute-start(f32[3,3,256]{2,1,0:T(4,128)S(1)} %bitcast.77), channel_id=1, source_target_pairs={{4,0},{8,4},{12,8},{16,12},{20,16},{24,20},{28,24},{5,1},{9,5},{13... | collective-permute-start | bytes 27656 | tf_op jit(solution)/shard_map/ppermute | solution.py:17
  218.2 9.1 %collective-permute-start.2 = (f32[3,256]{1,0:T(4,128)S(1)}, f32[3,256]{1,0:T(4,128)S(1)}, u32[]{:S(2)}, u32[]{:S(2)}) collective-permute-start(f32[3,256]{1,0:T(4,128)S(1)} %bitcast.78), channel_id=1, source_target_pairs={{0,1},{1,2},{2,3},{4,5},{5,6},{6,7},{8,9},{9,10},{10,11},{12,13},{... | collective-permute-start | bytes 9224 | tf_op jit(solution)/shard_map/ppermute | solution.py:17
  224.8 4.9 %collective-permute-start.3 = (f32[3,256]{1,0:T(4,128)S(1)}, f32[3,256]{1,0:T(4,128)S(1)}, u32[]{:S(2)}, u32[]{:S(2)}) collective-permute-start(f32[3,256]{1,0:T(4,128)S(1)} %bitcast.79), channel_id=1, source_target_pairs={{1,0},{2,1},{3,2},{5,4},{6,5},{7,6},{9,8},{10,9},{11,10},{13,12},{... | collective-permute-start | bytes 9224 | tf_op jit(solution)/shard_map/ppermute | solution.py:17
where the time goes:
time: 231 us; the launch traced here: 230 us
  matrix products  136 us (59%)
  local copies, waits for them, and re-layouts  40.2 us (17%)
  starting transfers between devices  18 us (8%)
  loops' own time  12 us (5%)
  other arithmetic  11.7 us (5%)
  waiting for transfers between devices  11.2 us (5%)
    dot_general x515, matrix products, accumulate(): jnp.dot(value_block, table, precision=lax.Precision.HIGHEST, preferred_el...  136 us
    another operation x2, loops' own time, onehot_sum(): result, unused = lax.scan(accumulate, start, (value_blocks, id_blocks))  11.7 us
    ppermute x4, starting transfers between devices, from_behind(): return lax.ppermute(array, axis, pairs)  11.6 us
    scatter x1, local copies, waits for them, and re-layouts, per_device(): outgoing = empty.at[:, slot_index].set(payload[:, sort_order])  10 us
    gather x1, local copies, waits for them, and re-layouts, per_device(): ranked = destination[sort_order]  8.39 us
    gather x11, local copies, waits for them, and re-layouts, per_device(): starts = jnp.searchsorted(ranked, jnp.arange(dom_count, dtype=jnp.int32))  6.99 us
    all_to_all x1, starting transfers between devices, per_device(): lax.all_to_all(outgoing, 'dom', split_axis=1, concat_axis=1, tiled=True)  6.35 us
    all_to_all x1, waiting for transfers between devices, per_device(): lax.all_to_all(outgoing, 'dom', split_axis=1, concat_axis=1, tiled=True)  5.68 us
  transfers between devices with their start and end apart: 5, of which 3 were waited for; matrix products, arithmetic and copies ran while one was open for 0% of the time, Pallas kernels for 0%

commit v1 on v0

--- a/solution.py
+++ b/solution.py
@@ -9,6 +9,18 @@
 PAIR_FIRST = np.array([0, 0, 0, 0, 1, 1, 1, 2, 2, 3], dtype=np.int32)
 PAIR_SECOND = np.array([0, 1, 2, 3, 1, 2, 3, 2, 3, 3], dtype=np.int32)
 GRAM_FROM_PAIR = np.array([0, 1, 2, 3, 1, 4, 5, 6, 2, 5, 7, 8, 3, 6, 8, 9], dtype=np.int32)
+
+
+def cut_along(x, dim, size):
+    shape = x.shape
+    parts = x.reshape(*shape[:dim], size, shape[dim] // size, *shape[dim + 1 :])
+    return jnp.moveaxis(parts, dim, 0)
+
+
+def laid_out(tiles, dim):
+    shape = list(tiles.shape[1:])
+    shape[dim] *= tiles.shape[0]
+    return jnp.moveaxis(tiles, 0, dim).reshape(shape)
 
 
 def from_behind(array, axis, by):
@@ -69,7 +81,15 @@
     payload = jnp.concatenate([weights, velocities, cell_float], axis=0)
     empty = jnp.zeros((payload.shape[0], slot_count), jnp.float32)
     outgoing = empty.at[:, slot_index].set(payload[:, sort_order])
-    arrived = lax.all_to_all(outgoing, "dom", split_axis=1, concat_axis=1, tiled=True)
+    size, index = (lax.axis_size("dom"), lax.axis_index("dom"))
+    blocks = cut_along(outgoing, 1, size)
+    out = blocks
+    for hop in range(1, size):
+        target, source = ((index + hop) % size, (index - hop) % size)
+        sent = lax.dynamic_index_in_dim(blocks, target, 0)
+        other = lax.ppermute(sent, "dom", [(i_2, (i_2 + hop) % size) for i_2 in range(size)])
+        out = lax.dynamic_update_slice_in_dim(out, other, source, axis=0)
+    arrived = laid_out(out, 1)
     products = expand_terms(arrived[:4], arrived[4:7])
     cell_index = arrived[7].astype(jnp.int32)
     totals = onehot_sum(products, cell_index, cell_count)

time: 231 us -> 231 us (level)
  waiting for transfers between devices: 11.2 us -> 3.26 us
  starting transfers between devices: 18 us -> 25.6 us
    ppermute x0 -> x7, starting transfers between devices: none -> 11.4 us  [per_device(): lax.ppermute(sent, 'dom', [(i_2, (i_2 + hop) % size) for i_2 in range(siz...]
    all_to_all x1 -> x0, starting transfers between devices: 6.35 us -> none  [per_device(): lax.all_to_all(outgoing, 'dom', split_axis=1, concat_axis=1, tiled=True)]
    all_to_all x1 -> x0, waiting for transfers between devices: 5.68 us -> none  [per_device(): lax.all_to_all(outgoing, 'dom', split_axis=1, concat_axis=1, tiled=True)]
    ppermute x4, starting transfers between devices: 11.6 us -> 14.2 us  [from_behind(): return lax.ppermute(array, axis, pairs)]
  transfers between devices with their start and end apart: 5 -> 11, of which waited for: 3 -> 2; matrix products, arithmetic and copies ran while one was open for 0% -> 1% of each run, Pallas kernels for 0% -> 0%
where the time goes in v1:
time: 231 us
  matrix products  136 us (59%)
  local copies, waits for them, and re-layouts  40.8 us (18%)
  starting transfers between devices  25.6 us (11%)
  loops' own time  12 us (5%)
  other arithmetic  11.6 us (5%)
  waiting for transfers between devices  3.26 us (1%)
    dot_general x515, matrix products, accumulate(): jnp.dot(value_block, table, precision=lax.Precision.HIGHEST, preferred_el...  136 us
    ppermute x4, starting transfers between devices, from_behind(): return lax.ppermute(array, axis, pairs)  14.2 us
    another operation x2, loops' own time, onehot_sum(): result, unused = lax.scan(accumulate, start, (value_blocks, id_blocks))  11.7 us
    ppermute x7, starting transfers between devices, per_device(): lax.ppermute(sent, 'dom', [(i_2, (i_2 + hop) % size) for i_2 in range(siz...  11.4 us
    scatter x1, local copies, waits for them, and re-layouts, per_device(): outgoing = empty.at[:, slot_index].set(payload[:, sort_order])  10 us
    gather x1, local copies, waits for them, and re-layouts, per_device(): ranked = destination[sort_order]  8.39 us
    gather x11, local copies, waits for them, and re-layouts, per_device(): starts = jnp.searchsorted(ranked, jnp.arange(dom_count, dtype=jnp.int32))  6.99 us
    gather x3, other arithmetic, per_device(): starts[ranked]  5.11 us
  transfers between devices with their start and end apart: 11, of which 2 were waited for; matrix products, arithmetic and copies ran while one was open for 1% of the time, Pallas kernels for 0%

profile of v1, /device:TPU:1, one launch (start us, length us, event | category | flops | bytes accessed | tf_op | source)
XLA Modules:
  0.0 231.0 jit_solution(15510239181098485924)
XLA Ops:
  0.7 0.7 reduce
  1.5 5.0 %sort.17 = (s32[1536]{0:T(1024)}, s32[1536]{0:T(1024)S(1)}) sort(s32[1536]{0:T(1024)S(1)} %reduce, s32[1536]{0:T(1024)S(1)} %iota.17), dimensions={0}, to_apply=%region_0.0 | sort | flops 16896 | bytes 24576 | tf_op jit(solution)/shard_map/jit(argsort)/sort | solution.py:74
  6.5 8.4 %gather_fusion.1 = s32[1536]{0:T(1024)S(1)} fusion(s32[1536]{0:T(1024)S(1)} %reduce, s32[2048]{0:T(1024)S(1)} %pad_clamp_fusion.1), kind=kCustom, calls=%fused_computation.1 | custom fusion | bytes 18432 | tf_op jit(solution)/shard_map/gather | solution.py:75
  15.0 7.6 %while.46 = (s32[]{:T(128)}, u32[8]{0:T(128)S(1)}, u32[8]{0:T(128)S(1)}, s32[1536]{0:T(1024)S(1)}, s32[]{:T(128)}, /*index=5*/s32[]{:T(128)}, s32[]{}) while((s32[]{:T(128)}, u32[8]{0:T(128)S(1)}, u32[8]{0:T(128)S(1)}, s32[1536]{0:T(1024)S(1)}, s32[]{:T(128)}, /*index=5*/s32[]{:T(128)}, s32[]{}) %tuple.97), condition=%wide.region_2.3_spmd.clone, body=%wide.region_1.2_spmd.clone.sunk | while | flops 1132 | bytes 4580 | solution.py:76
  22.6 0.7 fusion.27
  23.3 4.4 %fusion.20 = s32[1536]{0:T(1024)S(1)} fusion(s32[]{:T(128)} %bitcast.1, s32[]{:T(128)} %bitcast.2, s32[]{:T(128)} %bitcast.3, s32[]{:T(128)} %bitcast.4, s32[]{:T(128)} %bitcast.5, s32[]{:T(128)} %bitcast.7, s32[]{:T(128)} %bitcast.6, s32[1536]{0:T(1024)S(1)} %get-tuple-element.388), kind=kLoop, calls=%fused_computation.61 | loop fusion | flops 23040 | bytes 12316 | tf_op jit(solution)/shard_map/gather | solution.py:77
  27.8 0.7 broadcast_select_fusion.2
  28.9 10.0 %scatter_custom_fusion = f32[8,3072]{0,1:T(8,128)S(1)} fusion(s32[1536]{0:T(1024)S(1)} %fusion.21, f32[8,1536]{0,1:T(8,128)S(1)} %copy.76, s32[2048]{0:T(1024)S(1)} %pad_clamp_fusion.1, f32[]{:T(128)} %constant.165.clone.1), kind=kCustom, calls=%fused_computation.31 | custom fusion | bytes 98308 | tf_op jit(solution)/shard_map/scatter | solution.py:83
  39.1 2.1 collective-permute-start
  41.3 1.3 collective-permute-start.1
  42.7 2.3 %collective-permute-start.2 = (f32[1,8,384]{2,0,1:T(1,128)S(1)}, f32[1,8,384]{2,0,1:T(1,128)S(1)}, u32[]{:S(2)}, u32[]{:S(2)}) collective-permute-start(f32[1,8,384]{2,0,1:T(1,128)S(1)} %bitcast.98), channel_id=1, source_target_pairs={{0,12},{4,16},{8,20},{12,24},{16,28},{20,0},{24,4},{28,8},{1,13},{... | collective-permute-start | bytes 36872 | tf_op jit(solution)/shard_map/ppermute | solution.py:90
  45.1 1.0 collective-permute-start.3
  46.2 2.4 %collective-permute-start.4 = (f32[1,8,384]{2,0,1:T(1,128)S(1)}, f32[1,8,384]{2,0,1:T(1,128)S(1)}, u32[]{:S(2)}, u32[]{:S(2)}) collective-permute-start(f32[1,8,384]{2,0,1:T(1,128)S(1)} %bitcast.95), channel_id=1, source_target_pairs={{0,20},{4,24},{8,28},{12,0},{16,4},{20,8},{24,12},{28,16},{1,21},{... | collective-permute-start | bytes 36872 | tf_op jit(solution)/shard_map/ppermute | solution.py:90
  48.8 1.1 collective-permute-start.5
  49.9 1.2 collective-permute-start.6
  54.4 2.0 while.47
  57.2 0.8 reshape_reshape.3
  58.0 3.2 %copy.90 = f32[512,3,2]{1,2,0:T(2,128)S(1)} copy(f32[512,3,2]{2,0,1:T(8,128)S(1)} %bitcast.84) | data formatting | bytes 24576
  61.2 150.9 %while.48 = (s32[]{:T(128)}, f32[3,2304]{1,0:T(4,128)S(1)}, f32[512,3,2]{1,2,0:T(2,128)S(1)}, s32[512,2]{1,0:T(8,128)S(1)}, s32[]{:T(128)}, /*index=5*/s32[]{:T(128)}) while((s32[]{:T(128)}, f32[3,2304]{1,0:T(4,128)S(1)}, f32[512,3,2]{1,2,0:T(2,128)S(1)}, s32[512,2]{1,0:T(8,128)S(1)}, s32[]{:T(128)}, /*index=5*/s32[]{:T(128)}) %tuple.103), condition=%wide.region_10.11_spmd.clone, body=%wide.region_9.10_spmd.clone.sunk | while | flops 184323 | bytes 66151 | solution.py:63
  212.2 3.0 %collective-permute-start.7 = (f32[3,3,256]{2,1,0:T(4,128)S(1)}, f32[3,3,256]{2,1,0:T(4,128)S(1)}, u32[]{:S(2)}, u32[]{:S(2)}) collective-permute-start(f32[3,3,256]{2,1,0:T(4,128)S(1)} %bitcast.101), channel_id=1, source_target_pairs={{0,4},{4,8},{8,12},{12,16},{16,20},{20,24},{24,28},{1,5},{5,9},{9,... | collective-permute-start | bytes 27656 | tf_op jit(solution)/shard_map/ppermute | solution.py:29
  215.2 1.3 collective-permute-start.8
  216.6 3.1 %collective-permute-done.8 = f32[3,3,256]{2,1,0:T(4,128)S(1)} collective-permute-done((f32[3,3,256]{2,1,0:T(4,128)S(1)}, f32[3,3,256]{2,1,0:T(4,128)S(1)}, u32[]{:S(2)}, u32[]{:S(2)}) %collective-permute-start.8) | collective-permute-done | bytes 9248 | tf_op jit(solution)/shard_map/ppermute | solution.py:29
  219.7 6.8 %collective-permute-start.10 = (f32[3,256]{1,0:T(4,128)S(1)}, f32[3,256]{1,0:T(4,128)S(1)}, u32[]{:S(2)}, u32[]{:S(2)}) collective-permute-start(f32[3,256]{1,0:T(4,128)S(1)} %bitcast.103), channel_id=1, source_target_pairs={{1,0},{2,1},{3,2},{5,4},{6,5},{7,6},{9,8},{10,9},{11,10},{13,12},{... | collective-permute-start | bytes 9224 | tf_op jit(solution)/shard_map/ppermute | solution.py:29
  226.6 3.0 %collective-permute-start.9 = (f32[3,256]{1,0:T(4,128)S(1)}, f32[3,256]{1,0:T(4,128)S(1)}, u32[]{:S(2)}, u32[]{:S(2)}) collective-permute-start(f32[3,256]{1,0:T(4,128)S(1)} %bitcast.104), channel_id=1, source_target_pairs={{0,1},{1,2},{2,3},{4,5},{5,6},{6,7},{8,9},{9,10},{10,11},{12,13},{... | collective-permute-start | bytes 9224 | tf_op jit(solution)/shard_map/ppermute | solution.py:29
  (1179 shorter events, 154.7 us)
Async XLA Ops:
  14.9 13.5 %copy-start.1 = (f32[3,1,1536]{2,1,0:T(1,128)S(1)}, f32[3,1,1536]{2,1,0:T(1,128)}, u32[]{:S(2)}) copy-start(f32[3,1,1536]{2,1,0:T(1,128)} %param.19) | copy-start | bytes 55300
  14.9 13.6 %copy-start = (f32[4,1,1536]{2,1,0:T(1,128)S(1)}, f32[4,1,1536]{2,1,0:T(1,128)}, u32[]{:S(2)}) copy-start(f32[4,1,1536]{2,1,0:T(1,128)} %param.18) | copy-start | bytes 73732
  14.9 13.6 %copy-start.3 = (s32[1,1536]{1,0:T(1,128)S(1)}, s32[1,1536]{1,0:T(1,128)}, u32[]{:S(2)}) copy-start(s32[1,1536]{1,0:T(1,128)} %param.21) | copy-start | bytes 18436
  38.9 9.7 %copy-start.7 = (s32[10]{0:T(128)S(1)}, s32[10]{0:T(128)}, u32[]{:S(2)}) copy-start(s32[10]{0:T(128)} %constant.210) | copy-start | bytes 124
  38.9 9.7 %copy-start.6 = (s32[10]{0:T(128)S(1)}, s32[10]{0:T(128)}, u32[]{:S(2)}) copy-start(s32[10]{0:T(128)} %constant.211) | copy-start | bytes 124
  38.9 12.2 %copy-start.5 = (s32[16]{0:T(128)S(1)}, s32[16]{0:T(128)}, u32[]{:S(2)}) copy-start(s32[16]{0:T(128)} %constant.212) | copy-start | bytes 196
  39.1 9.7 %collective-permute-start = (f32[1,8,384]{2,0,1:T(1,128)S(1)}, f32[1,8,384]{2,0,1:T(1,128)S(1)}, u32[]{:S(2)}, u32[]{:S(2)}) collective-permute-start(f32[1,8,384]{2,0,1:T(1,128)S(1)} %bitcast.100), channel_id=1, source_target_pairs={{0,4},{4,8},{8,12},{12,16},{16,20},{20,24},{24,28},{28,0},{1,5},{5... | collective-permute-start | bytes 36872 | tf_op jit(solution)/shard_map/ppermute | solution.py:90
  41.2 10.5 %copy-start.2 = (f32[16,1,256]{2,1,0:T(1,128)S(1)}, f32[16,1,256]{2,1,0:T(1,128)}, u32[]{:S(2)}) copy-start(f32[16,1,256]{2,1,0:T(1,128)} %param.22) | copy-start | bytes 49156
  41.2 10.5 %copy-start.4 = (s32[4,1,256]{2,1,0:T(1,128)S(1)}, s32[4,1,256]{2,1,0:T(1,128)}, u32[]{:S(2)}) copy-start(s32[4,1,256]{2,1,0:T(1,128)} %param.23) | copy-start | bytes 12292
  41.3 8.6 %collective-permute-start.1 = (f32[1,8,384]{2,0,1:T(1,128)S(1)}, f32[1,8,384]{2,0,1:T(1,128)S(1)}, u32[]{:S(2)}, u32[]{:S(2)}) collective-permute-start(f32[1,8,384]{2,0,1:T(1,128)S(1)} %bitcast.99), channel_id=1, source_target_pairs={{0,8},{4,12},{8,16},{12,20},{16,24},{20,28},{24,0},{28,4},{1,9},{5... | collective-permute-start | bytes 36872 | tf_op jit(solution)/shard_map/ppermute | solution.py:90
  42.7 9.5 %collective-permute-start.2 = (f32[1,8,384]{2,0,1:T(1,128)S(1)}, f32[1,8,384]{2,0,1:T(1,128)S(1)}, u32[]{:S(2)}, u32[]{:S(2)}) collective-permute-start(f32[1,8,384]{2,0,1:T(1,128)S(1)} %bitcast.98), channel_id=1, source_target_pairs={{0,12},{4,16},{8,20},{12,24},{16,28},{20,0},{24,4},{28,8},{1,13},{... | collective-permute-start | bytes 36872 | tf_op jit(solution)/shard_map/ppermute | solution.py:90
  45.1 7.2 %collective-permute-start.3 = (f32[1,8,384]{2,0,1:T(1,128)S(1)}, f32[1,8,384]{2,0,1:T(1,128)S(1)}, u32[]{:S(2)}, u32[]{:S(2)}) collective-permute-start(f32[1,8,384]{2,0,1:T(1,128)S(1)} %bitcast.96), channel_id=1, source_target_pairs={{0,16},{4,20},{8,24},{12,28},{16,0},{20,4},{24,8},{28,12},{1,17},{... | collective-permute-start | bytes 36872 | tf_op jit(solution)/shard_map/ppermute | solution.py:90
  46.2 6.2 %collective-permute-start.4 = (f32[1,8,384]{2,0,1:T(1,128)S(1)}, f32[1,8,384]{2,0,1:T(1,128)S(1)}, u32[]{:S(2)}, u32[]{:S(2)}) collective-permute-start(f32[1,8,384]{2,0,1:T(1,128)S(1)} %bitcast.95), channel_id=1, source_target_pairs={{0,20},{4,24},{8,28},{12,0},{16,4},{20,8},{24,12},{28,16},{1,21},{... | collective-permute-start | bytes 36872 | tf_op jit(solution)/shard_map/ppermute | solution.py:90
  48.8 3.7 %collective-permute-start.5 = (f32[1,8,384]{2,0,1:T(1,128)S(1)}, f32[1,8,384]{2,0,1:T(1,128)S(1)}, u32[]{:S(2)}, u32[]{:S(2)}) collective-permute-start(f32[1,8,384]{2,0,1:T(1,128)S(1)} %bitcast.97), channel_id=1, source_target_pairs={{0,24},{4,28},{8,0},{12,4},{16,8},{20,12},{24,16},{28,20},{1,25},{... | collective-permute-start | bytes 36872 | tf_op jit(solution)/shard_map/ppermute | solution.py:90
  49.9 2.7 %collective-permute-start.6 = (f32[1,8,384]{2,0,1:T(1,128)S(1)}, f32[1,8,384]{2,0,1:T(1,128)S(1)}, u32[]{:S(2)}, u32[]{:S(2)}) collective-permute-start(f32[1,8,384]{2,0,1:T(1,128)S(1)} %bitcast.94), channel_id=1, source_target_pairs={{0,28},{4,0},{8,4},{12,8},{16,12},{20,16},{24,20},{28,24},{1,29},{... | collective-permute-start | bytes 36872 | tf_op jit(solution)/shard_map/ppermute | solution.py:90
  212.2 4.3 %collective-permute-start.7 = (f32[3,3,256]{2,1,0:T(4,128)S(1)}, f32[3,3,256]{2,1,0:T(4,128)S(1)}, u32[]{:S(2)}, u32[]{:S(2)}) collective-permute-start(f32[3,3,256]{2,1,0:T(4,128)S(1)} %bitcast.101), channel_id=1, source_target_pairs={{0,4},{4,8},{8,12},{12,16},{16,20},{20,24},{24,28},{1,5},{5,9},{9,... | collective-permute-start | bytes 27656 | tf_op jit(solution)/shard_map/ppermute | solution.py:29
  215.2 4.4 %collective-permute-start.8 = (f32[3,3,256]{2,1,0:T(4,128)S(1)}, f32[3,3,256]{2,1,0:T(4,128)S(1)}, u32[]{:S(2)}, u32[]{:S(2)}) collective-permute-start(f32[3,3,256]{2,1,0:T(4,128)S(1)} %bitcast.102), channel_id=1, source_target_pairs={{4,0},{8,4},{12,8},{16,12},{20,16},{24,20},{28,24},{5,1},{9,5},{13... | collective-permute-start | bytes 27656 | tf_op jit(solution)/shard_map/ppermute | solution.py:29
  219.7 10.5 %collective-permute-start.10 = (f32[3,256]{1,0:T(4,128)S(1)}, f32[3,256]{1,0:T(4,128)S(1)}, u32[]{:S(2)}, u32[]{:S(2)}) collective-permute-start(f32[3,256]{1,0:T(4,128)S(1)} %bitcast.103), channel_id=1, source_target_pairs={{1,0},{2,1},{3,2},{5,4},{6,5},{7,6},{9,8},{10,9},{11,10},{13,12},{... | collective-permute-start | bytes 9224 | tf_op jit(solution)/shard_map/ppermute | solution.py:29
  226.6 3.8 %collective-permute-start.9 = (f32[3,256]{1,0:T(4,128)S(1)}, f32[3,256]{1,0:T(4,128)S(1)}, u32[]{:S(2)}, u32[]{:S(2)}) collective-permute-start(f32[3,256]{1,0:T(4,128)S(1)} %bitcast.104), channel_id=1, source_target_pairs={{0,1},{1,2},{2,3},{4,5},{5,6},{6,7},{8,9},{9,10},{10,11},{12,13},{... | collective-permute-start | bytes 9224 | tf_op jit(solution)/shard_map/ppermute | solution.py:29
